TPU v7x, 32 devices: a whole 2x2x4 slice. The times are simulated.
32 devices in a mesh: groups: 2 (over x), seq: 16 (over z, y, core).
Axes of the slice: x: 2, y: 2, z: 4, core: 2. Of those that a mesh axis runs over, the one named last changes fastest.
Arguments:
- signal: bfloat16 [16384, 2048], P(('groups', 'seq')), parts along dimension 0, may hold values from -6 to 6
- gate_input: bfloat16 [16384, 2048], P(('groups', 'seq')), parts along dimension 0, may hold values from -6 to 6
- cotangent: bfloat16 [16384, 2048], P(('groups', 'seq')), parts along dimension 0, may hold values from -6 to 6
- block_factor: bfloat16 [512, 512], replicated, may hold values from -0.25 to 0.25
- cross_factor: bfloat16 [512, 16, 16], P('seq'), may hold values from -1.5 to 1.5
- order_table: int32 [512], replicated, may hold values from 0 to 511, each once
Outputs:
- grad_signal: bfloat16 [16384, 2048], P(('groups', 'seq')), parts along dimension 0
- grad_gate: bfloat16 [16384, 2048], P(('groups', 'seq')), parts along dimension 0
- grad_block: float32 [1024, 512], P('groups'), parts along dimension 0
- grad_cross: float32 [512, 32, 16], P('seq', 'groups'), parts along dimension 1
There are 2 independent parts, one for each index of `groups`. A program takes and returns all parts, laid end to end along the dimension named above; an argument that names none is the same for every part. Nothing has to cross between parts.
Inputs may be any that keep to these rules, and one draw needn't show every extreme that they name: order_table holds every number of 0 to 511 exactly once.
All inputs are finite; a program needn't handle non-finite values.
Results may differ from a plain program's by a relative error of at most 0.0057.
Values may be sent and summed in bfloat16 or wider, within the bound.
A program may use at most 64 MiB of HBM per device.

v0:
```python
import math
import jax
import jax.numpy as jnp
from jax import lax
from jax.sharding import PartitionSpec as P


def per_device(signal, gate_input, cotangent, block_factor, cross_factor, order_table):
    f32 = jnp.float32
    bf16 = jnp.bfloat16
    count = lax.axis_size("seq")
    width = signal.shape[1]
    permuted = jnp.take(signal, order_table, axis=0)
    mixed = jnp.dot(block_factor, permuted, preferred_element_type=f32).astype(bf16)
    gate_grad = (cotangent.astype(f32) * gate_input.astype(f32)).astype(bf16)
    spread_mixed = lax.all_to_all(mixed[None], "seq", split_axis=1, concat_axis=0, tiled=True)
    spread_grad = lax.all_to_all(gate_grad[None], "seq", split_axis=1, concat_axis=0, tiled=True)
    gated = jnp.einsum(
        "cij,jcd->icd", cross_factor, spread_mixed, preferred_element_type=f32
    ).astype(bf16)
    gated_home = lax.all_to_all(gated, "seq", split_axis=0, concat_axis=1, tiled=True)
    grad_cross = jnp.einsum(
        "icd,jcd->cij", spread_grad, spread_mixed, preferred_element_type=f32
    ) / math.sqrt(width)
    back = jnp.einsum("cij,icd->jcd", cross_factor, spread_grad, preferred_element_type=f32).astype(
        bf16
    )
    back_home = lax.all_to_all(back, "seq", split_axis=0, concat_axis=1, tiled=True)
    grad_gate = (cotangent.astype(f32) * gated_home[0].astype(f32)).astype(bf16)
    back_rows = back_home[0]
    partial_block = lax.dot_general(
        back_rows, permuted, (((1,), (1,)), ((), ())), preferred_element_type=f32
    )
    grad_block = lax.psum(partial_block, "seq") / math.sqrt(count * width)
    spread = lax.dot_general(
        block_factor, back_rows, (((0,), (0,)), ((), ())), preferred_element_type=f32
    ).astype(bf16)
    grad_signal = jnp.zeros_like(spread).at[order_table].set(spread)
    return (grad_signal, grad_gate, grad_block, grad_cross)


def solution(mesh):
    in_specs = (
        P(("groups", "seq"), None),
        P(("groups", "seq"), None),
        P(("groups", "seq"), None),
        P(),
        P("seq", None, None),
        P(),
    )
    out_specs = (
        P(("groups", "seq"), None),
        P(("groups", "seq"), None),
        P("groups", None),
        P("seq", "groups", None),
    )
    return jax.shard_map(
        per_device, mesh=mesh, in_specs=in_specs, out_specs=out_specs, check_vma=False
    )
```

profile of v0, /device:TPU:0, one launch (start us, length us, event | category | flops | bytes accessed | tf_op | source)
XLA Modules:
  0.0 409.7 jit_solution(3647754906035799778)
XLA Ops:
  7.2 0.0 copy-start
  7.2 0.8 compare_and_fusion
  8.0 0.7 compare_select_fusion
  8.7 0.1 copy-done
  8.8 0.0 copy-start.10
  8.8 3.3 gather_fusion
  12.1 0.0 copy-done.10
  12.1 3.1 fusion.3
  15.1 7.7 %copy.32 = bf16[1,512,2048]{2,0,1:T(2,128)(2,1)} copy(bf16[1,512,2048]{1,2,0:T(8,128)(2,1)S(1)} %fusion.3) | data formatting | bytes 4194304 | tf_op jit(solution)/shard_map/broadcast_in_dim | solution.py:16
  22.9 0.5 broadcast.9
  23.4 13.2 %reduce = bf16[512,2048]{1,0:T(8,128)(2,1)S(1)} reduce(bf16[512,1,2048]{2,1,0:T(2,128)(2,1)} %bitcast.31, bf16[]{:T(256)} %broadcast.9), dimensions={1}, to_apply=%bitcast.20.reduce_sub_computation | reduce | bytes 4194306
  36.5 2.8 reshape.52
  39.3 0.0 copy-start.9
  39.3 7.5 %all-to-all-start.2 = ((bf16[16,2,32768]{2,1,0:T(2,128)(2,1)}), bf16[16,2,32768]{2,1,0:T(2,128)(2,1)S(1)}, u32[]{:S(2)}, u32[]{:S(2)}) async-start(bf16[16,2,32768]{2,1,0:T(2,128)(2,1)} %reshape.52), calls=%async_computation.2 | async-start | bytes 4194304 | tf_op jit(solution)/shard_map/all_to_all | solution.py:16
  46.8 0.0 all-reduce.2.cloned.1.call-start
  46.9 0.0 copy-done.9
  46.9 0.2 copy.34
  47.1 40.9 %all-to-all-done.2 = bf16[16,2,32768]{2,1,0:T(2,128)(2,1)S(1)} async-done(((bf16[16,2,32768]{2,1,0:T(2,128)(2,1)}), bf16[16,2,32768]{2,1,0:T(2,128)(2,1)S(1)}, u32[]{:S(2)}, u32[]{:S(2)}) %all-to-all-start.2) | async-done | bytes 2097184 | tf_op jit(solution)/shard_map/all_to_all | solution.py:16
  87.9 6.7 %reshape.53 = bf16[512,1,2048]{2,1,0:T(2,128)(2,1)} reshape(bf16[16,2,32768]{2,1,0:T(2,128)(2,1)S(1)} %all-to-all-done.2) | data formatting | bytes 4194304
  94.7 3.5 copy.40
  98.1 0.0 copy-start.2
  98.1 2.4 fusion.5
  100.6 0.0 copy-done.2
  100.6 1.2 copy.35
  101.7 0.0 copy-start.5
  101.8 0.0 copy-start.6
  101.8 58.6 %all_to_all.42 = bf16[16,32,2048]{2,1,0:T(8,128)(2,1)S(1)} all-to-all(bf16[16,32,2048]{2,1,0:T(8,128)(2,1)S(1)} %copy.35), channel_id=1, replica_groups=mesh['groups'=2,'seq'=16] {'seq'}, dimensions={0} | all-to-all | bytes 4194304 | tf_op jit(solution)/shard_map/all_to_all | solution.py:21
  160.4 0.0 copy-done.5
  160.4 0.0 copy-done.6
  160.4 3.0 fusion.1
  163.3 5.2 %copy.54 = bf16[1,512,2048]{2,0,1:T(2,128)(2,1)} copy(bf16[1,512,2048]{2,1,0:T(8,128)(2,1)S(1)} %get-tuple-element.17) | data formatting | bytes 4194304 | tf_op jit(solution)/shard_map/broadcast_in_dim | solution.py:17
  168.5 13.2 %reduce.1 = bf16[512,2048]{1,0:T(8,128)(2,1)S(1)} reduce(bf16[512,1,2048]{2,1,0:T(2,128)(2,1)} %bitcast.32, bf16[]{:T(256)} %broadcast.9), dimensions={1}, to_apply=%bitcast.29.reduce_sub_computation | reduce | bytes 4194306
  181.7 2.8 reshape.50
  184.4 52.4 %all_to_all.43 = bf16[16,2,32768]{2,1,0:T(2,128)(2,1)S(1)} all-to-all(bf16[16,2,32768]{2,1,0:T(2,128)(2,1)} %reshape.50), channel_id=1, replica_groups=mesh['groups'=2,'seq'=16] {'seq'}, dimensions={0} | all-to-all | bytes 4194304 | tf_op jit(solution)/shard_map/all_to_all | solution.py:17
  236.9 6.7 %reshape.51 = bf16[512,1,2048]{2,1,0:T(2,128)(2,1)} reshape(bf16[16,2,32768]{2,1,0:T(2,128)(2,1)S(1)} %all_to_all.43) | data formatting | bytes 4194304
  243.6 3.5 copy.39
  247.1 0.0 copy-start.4
  247.1 2.4 fusion.4
  249.5 0.0 copy-done.4
  249.5 1.2 copy.30
  250.6 0.0 copy-start.7
  250.7 52.4 %all_to_all.44 = bf16[16,32,2048]{2,1,0:T(8,128)(2,1)S(1)} all-to-all(bf16[16,32,2048]{2,1,0:T(8,128)(2,1)S(1)} %copy.30), channel_id=1, replica_groups=mesh['groups'=2,'seq'=16] {'seq'}, dimensions={0} | all-to-all | bytes 4194304 | tf_op jit(solution)/shard_map/all_to_all | solution.py:28
  303.0 0.0 copy-start.8
  303.0 1.4 copy-done.8
  304.4 0.0 copy-done.7
  304.4 0.0 copy-start.3
  304.4 2.3 fusion.19
  306.7 0.0 all-reduce.2.cloned.1.call-update
  306.7 0.0 copy-done.3
  306.7 3.9 fusion.12
  310.6 0.8 copy.38
  311.5 4.3 %fusion.2 = bf16[512,2048]{0,1:T(8,128)(2,1)} fusion(bf16[512,2048]{1,0:T(8,128)(2,1)} %bitcast.40, bf16[512,512]{1,0:T(8,128)(2,1)S(1)} %copy-done.10), kind=kOutput, calls=%fused_computation.10 | convolution fusion | flops 1074790400 | bytes 4718592 | tf_op jit(solution)/shard_map/dot_general | solution.py:35
  315.8 0.0 copy-start.1
  315.8 4.1 %copy.31 = bf16[512,2048]{1,0:T(8,128)(2,1)} copy(bf16[512,2048]{0,1:T(8,128)(2,1)} %fusion.2) | data formatting | bytes 4194304 | tf_op jit(solution)/shard_map/convert_element_type | solution.py:37
  319.9 6.1 %scatter_custom_fusion = bf16[512,2048]{1,0:T(8,128)(2,1)} fusion(s32[512]{0:T(512)S(1)} %compare_select_fusion, bf16[512,2048]{1,0:T(8,128)(2,1)} %copy.31, bf16[]{:T(256)} %constant.8.clone.1), kind=kCustom, calls=%fused_computation.22 | custom fusion | bytes 2097664 | tf_op jit(solution)/shard_map/scatter | solution.py:38
  326.0 74.5 %all-reduce.2.cloned.1.call-done = f32[512,512]{1,0:T(8,128)} async-done(((f32[512,512]{1,0:T(8,128)}), f32[512,512]{1,0:T(8,128)}) %all-reduce.2.cloned.1.call-update) | async-done | bytes 1048592 | tf_op jit(solution)/shard_map/psum | solution.py:34
  400.6 2.3 broadcast_multiply_fusion
  402.9 0.0 copy-done.1
  (1 shorter events, 0.0 us)
Async XLA Ops:
  7.2 1.6 copy-start
  8.8 3.3 copy-start.10
  39.3 7.6 %copy-start.9 = (bf16[32,16,16]{0,2,1:T(8,128)(2,1)S(1)}, bf16[32,16,16]{0,2,1:T(8,128)(2,1)}, u32[]{:S(2)}) copy-start(bf16[32,16,16]{0,2,1:T(8,128)(2,1)} %param.10) | copy-start | bytes 49156
  39.3 48.6 %all-to-all-start.2 = ((bf16[16,2,32768]{2,1,0:T(2,128)(2,1)}), bf16[16,2,32768]{2,1,0:T(2,128)(2,1)S(1)}, u32[]{:S(2)}, u32[]{:S(2)}) async-start(bf16[16,2,32768]{2,1,0:T(2,128)(2,1)} %reshape.52), calls=%async_computation.2 | async-start | bytes 4194304 | tf_op jit(solution)/shard_map/all_to_all | solution.py:16
  46.8 353.7 %all-reduce.2.cloned.1.call-start = ((), (), s32[]{:S(2)}) async-start(), calls=%async_computation.4 | async-start | bytes 2097152 | tf_op jit(solution)/shard_map/psum | solution.py:34
  98.1 2.4 copy-start.2
  101.7 58.6 %copy-start.5 = (bf16[512,2048]{1,0:T(8,128)(2,1)S(1)}, bf16[512,2048]{1,0:T(8,128)(2,1)}, u32[]{:S(2)}) copy-start(bf16[512,2048]{1,0:T(8,128)(2,1)} %param.8) | copy-start | bytes 6291460
  101.8 58.6 %copy-start.6 = (bf16[512,2048]{1,0:T(8,128)(2,1)S(1)}, bf16[512,2048]{1,0:T(8,128)(2,1)}, u32[]{:S(2)}) copy-start(bf16[512,2048]{1,0:T(8,128)(2,1)} %param.7) | copy-start | bytes 6291460
  247.1 2.4 copy-start.4
  250.6 53.7 %copy-start.7 = (bf16[512,2048]{1,0:T(8,128)(2,1)S(1)}, bf16[512,2048]{1,0:T(8,128)(2,1)}, u32[]{:S(2)}) copy-start(bf16[512,2048]{1,0:T(8,128)(2,1)} %gather_fusion) | copy-start | bytes 6291460
  303.0 1.4 copy-start.8
  304.4 2.4 copy-start.3
  315.8 87.1 %copy-start.1 = (bf16[512,2048]{1,0:T(8,128)(2,1)S(1)}, bf16[512,2048]{1,0:T(8,128)(2,1)}, u32[]{:S(2)}) copy-start(bf16[512,2048]{1,0:T(8,128)(2,1)} %param.6) | copy-start | bytes 6291460
Sparse Core Ops, SparseCore 0:
  306.9 93.6 all-reduce.1
where the time goes:
time: 410 us
  blocking collectives  163 us (40%)
  waiting for transfers between devices  115 us (28%)
  local copies, waits for them, and re-layouts  57.6 us (14%)
  other arithmetic  33.1 us (8%)
  matrix products  18.5 us (5%)
  between operations  14.2 us (3%)
  starting transfers between devices  7.56 us (2%)
    psum x1, waiting for transfers between devices, per_device(): grad_block = lax.psum(partial_block, 'seq') / math.sqrt(count * width)  74.5 us
    all_to_all x1, blocking collectives, per_device(): lax.all_to_all(gated, 'seq', split_axis=0, concat_axis=1, tiled=True)  58.6 us
    all_to_all x1, blocking collectives, per_device(): lax.all_to_all(gate_grad[None], 'seq', split_axis=1, concat_axis=0, tiled...  52.4 us
    all_to_all x1, blocking collectives, per_device(): lax.all_to_all(back, 'seq', split_axis=0, concat_axis=1, tiled=True)  52.4 us
    all_to_all x1, waiting for transfers between devices, per_device(): lax.all_to_all(mixed[None], 'seq', split_axis=1, concat_axis=0, tiled=True)  40.9 us
    unnamed x31, local copies, waits for them, and re-layouts  28.9 us
    unnamed x2, other arithmetic  26.3 us
  transfers between devices with their start and end apart: 2, of which 2 were waited for; matrix products, arithmetic and copies ran while one was open for 5% of the time, Pallas kernels for 0%

commit v1 on v0

--- a/solution.py
+++ b/solution.py
@@ -3,6 +3,22 @@
 import jax.numpy as jnp
 from jax import lax
 from jax.sharding import PartitionSpec as P
+
+
+def settle_the_corner(patch, array_axis, page):
+    z_new = patch.shape
+    all_values = patch.reshape(
+        *z_new[:array_axis], page, z_new[array_axis] // page, *z_new[array_axis + 1 :]
+    )
+    left_arr = jnp.moveaxis(all_values, array_axis, 0)
+    return left_arr
+
+
+def _recover_hubs(local_block, axis_no):
+    main = list(local_block.shape[1:])
+    main[axis_no] *= local_block.shape[0]
+    part_next = jnp.moveaxis(local_block, 0, axis_no).reshape(main)
+    return part_next
 
 
 def per_device(signal, gate_input, cotangent, block_factor, cross_factor, order_table):
@@ -18,7 +34,18 @@
     gated = jnp.einsum(
         "cij,jcd->icd", cross_factor, spread_mixed, preferred_element_type=f32
     ).astype(bf16)
-    gated_home = lax.all_to_all(gated, "seq", split_axis=0, concat_axis=1, tiled=True)
+    block_out = jax.lax.psum(1, "seq")
+    arr_next, shaped = (block_out, jax.lax.axis_index("seq"))
+    upper = settle_the_corner(gated, 0, arr_next)
+    clean = upper
+    for k0 in tuple(range(1, arr_next)):
+        then, q_next = ((shaped + k0) % arr_next, (shaped - k0) % arr_next)
+        mixed_arr = lax.dynamic_index_in_dim(upper, then, 0)
+        v1 = jax.lax.ppermute(
+            mixed_arr, "seq", [(nth, (nth + k0) % arr_next) for nth in range(arr_next)]
+        )
+        clean = lax.dynamic_update_slice_in_dim(clean, v1, q_next, axis=0)
+    gated_home = _recover_hubs(clean, 1)
     grad_cross = jnp.einsum(
         "icd,jcd->cij", spread_grad, spread_mixed, preferred_element_type=f32
     ) / math.sqrt(width)

time: 410 us -> 525 us (1.28); the launches traced: 410 us -> 515 us
  local copies, waits for them, and re-layouts: 57.6 us -> 130 us
  blocking collectives: 163 us -> 103 us
  starting transfers between devices: 7.56 us -> 56.5 us
  waiting for transfers between devices: 115 us -> 158 us
    dynamic_update_slice x0 -> x15, local copies, waits for them, and re-layouts: none -> 64.2 us  [per_device(): clean = lax.dynamic_update_slice_in_dim(clean, v1, q_next, axis=0)]
    all_to_all x1 -> x0, blocking collectives: 58.6 us -> none  [per_device(): lax.all_to_all(gated, 'seq', split_axis=0, concat_axis=1, tiled=True)]
    ppermute x0 -> x15, starting transfers between devices: none -> 48.5 us  [per_device(): jax.lax.ppermute(mixed_arr, 'seq', [(nth, (nth + k0) % arr_next) for nth...]
    ppermute x0 -> x15, waiting for transfers between devices: none -> 43.7 us  [per_device(): jax.lax.ppermute(mixed_arr, 'seq', [(nth, (nth + k0) % arr_next) for nth...]
    unnamed x31 -> x53, local copies, waits for them, and re-layouts: 28.9 us -> 32 us
  transfers between devices with their start and end apart: 2 -> 17, of which waited for: 2 -> 8; matrix products, arithmetic and copies ran while one was open for 5% -> 15% of each run, Pallas kernels for 0% -> 0%
where the time goes in v1:
time: 525 us; the launch traced here: 515 us
  waiting for transfers between devices  158 us (30%)
  local copies, waits for them, and re-layouts  130 us (25%)
  blocking collectives  103 us (20%)
  starting transfers between devices  56.5 us (11%)
  other arithmetic  32.9 us (6%)
  matrix products  18.5 us (4%)
  between operations  15.3 us (3%)
    psum x1, waiting for transfers between devices, per_device(): grad_block = lax.psum(partial_block, 'seq') / math.sqrt(count * width)  74.5 us
    dynamic_update_slice x15, local copies, waits for them, and re-layouts, per_device(): clean = lax.dynamic_update_slice_in_dim(clean, v1, q_next, axis=0)  64.2 us
    all_to_all x1, blocking collectives, per_device(): lax.all_to_all(back, 'seq', split_axis=0, concat_axis=1, tiled=True)  52.2 us
    all_to_all x1, blocking collectives, per_device(): lax.all_to_all(gate_grad[None], 'seq', split_axis=1, concat_axis=0, tiled...  51.2 us
    ppermute x15, starting transfers between devices, per_device(): jax.lax.ppermute(mixed_arr, 'seq', [(nth, (nth + k0) % arr_next) for nth...  48.5 us
    ppermute x15, waiting for transfers between devices, per_device(): jax.lax.ppermute(mixed_arr, 'seq', [(nth, (nth + k0) % arr_next) for nth...  43.7 us
    all_to_all x1, waiting for transfers between devices, per_device(): lax.all_to_all(mixed[None], 'seq', split_axis=1, concat_axis=0, tiled=True)  40.1 us
    unnamed x53, local copies, waits for them, and re-layouts  32 us
  transfers between devices with their start and end apart: 17, of which 8 were waited for; matrix products, arithmetic and copies ran while one was open for 15% of the time, Pallas kernels for 0%

profile of v1, /device:TPU:0, one launch (start us, length us, event | category | flops | bytes accessed | tf_op | source)
XLA Modules:
  0.0 514.9 jit_solution(10524530545125910067)
XLA Ops:
  7.2 0.8 compare_and_fusion
  8.0 0.7 compare_select_fusion
  8.8 3.3 gather_fusion
  12.1 3.1 fusion.3
  15.1 7.7 %copy.32 = bf16[1,512,2048]{2,0,1:T(2,128)(2,1)} copy(bf16[1,512,2048]{1,2,0:T(8,128)(2,1)S(1)} %fusion.3) | data formatting | bytes 4194304 | tf_op jit(solution)/shard_map/broadcast_in_dim | solution.py:32
  22.9 0.5 broadcast.39
  23.4 13.2 %reduce = bf16[512,2048]{1,0:T(8,128)(2,1)S(1)} reduce(bf16[512,1,2048]{2,1,0:T(2,128)(2,1)} %bitcast.62, bf16[]{:T(256)} %broadcast.39), dimensions={1}, to_apply=%bitcast.48.reduce_sub_computation | reduce | bytes 4194306
  36.5 2.8 reshape.95
  39.3 7.5 %all-to-all-start.2 = ((bf16[16,2,32768]{2,1,0:T(2,128)(2,1)}), bf16[16,2,32768]{2,1,0:T(2,128)(2,1)S(1)}, u32[]{:S(2)}, u32[]{:S(2)}) async-start(bf16[16,2,32768]{2,1,0:T(2,128)(2,1)} %reshape.95), calls=%async_computation.2 | async-start | bytes 4194304 | tf_op jit(solution)/shard_map/all_to_all | solution.py:32
  47.8 40.1 %all-to-all-done.2 = bf16[16,2,32768]{2,1,0:T(2,128)(2,1)S(1)} async-done(((bf16[16,2,32768]{2,1,0:T(2,128)(2,1)}), bf16[16,2,32768]{2,1,0:T(2,128)(2,1)S(1)}, u32[]{:S(2)}, u32[]{:S(2)}) %all-to-all-start.2) | async-done | bytes 2097184 | tf_op jit(solution)/shard_map/all_to_all | solution.py:32
  87.9 6.8 %reshape.96 = bf16[512,1,2048]{2,1,0:T(2,128)(2,1)} reshape(bf16[16,2,32768]{2,1,0:T(2,128)(2,1)S(1)} %all-to-all-done.2) | data formatting | bytes 4194304
  94.7 3.5 copy.40
  98.2 1.4 copy-done.2
  99.5 2.4 convolution_convert_fusion
  102.0 5.0 dynamic-slice_bitcast_fusion
  107.0 8.6 %collective-permute-start.9 = (bf16[1,1,32,2048]{3,0,2,1:T(2,128)(2,1)S(1)}, bf16[1,1,32,2048]{3,0,2,1:T(2,128)(2,1)S(1)}, u32[]{:S(2)}, u32[]{:S(2)}) collective-permute-start(bf16[1,1,32,2048]{3,0,2,1:T(2,128)(2,1)S(1)} %get-tuple-element.23), channel_id=1, source_target_pairs={{0,10},{1,11},{2,12},{3,13},{4,14},{5,15},{6,0},{7,1},{8,2},{9,3},... | collective-permute-start | bytes 393224 | tf_op jit(solution)/shard_map/ppermute | solution.py:44
  115.7 1.8 collective-permute-start.7
  117.5 1.4 collective-permute-start.6
  118.8 3.8 collective-permute-start.5
  123.1 18.6 %collective-permute-start.4 = (bf16[1,1,32,2048]{3,0,2,1:T(2,128)(2,1)S(1)}, bf16[1,1,32,2048]{3,0,2,1:T(2,128)(2,1)S(1)}, u32[]{:S(2)}, u32[]{:S(2)}) collective-permute-start(bf16[1,1,32,2048]{3,0,2,1:T(2,128)(2,1)S(1)} %get-tuple-element.28), channel_id=1, source_target_pairs={{0,5},{1,6},{2,7},{3,8},{4,9},{5,10},{6,11},{7,12},{8,13},{9,14},{... | collective-permute-start | bytes 393224 | tf_op jit(solution)/shard_map/ppermute | solution.py:44
  141.7 13.3 %collective-permute-start.3 = (bf16[1,1,32,2048]{3,0,2,1:T(2,128)(2,1)S(1)}, bf16[1,1,32,2048]{3,0,2,1:T(2,128)(2,1)S(1)}, u32[]{:S(2)}, u32[]{:S(2)}) collective-permute-start(bf16[1,1,32,2048]{3,0,2,1:T(2,128)(2,1)S(1)} %get-tuple-element.29), channel_id=1, source_target_pairs={{0,4},{1,5},{2,6},{3,7},{4,8},{5,9},{6,10},{7,11},{8,12},{9,13},{1... | collective-permute-start | bytes 393224 | tf_op jit(solution)/shard_map/ppermute | solution.py:44
  155.0 19.1 %collective-permute-done.7 = bf16[1,1,32,2048]{3,0,2,1:T(2,128)(2,1)S(1)} collective-permute-done((bf16[1,1,32,2048]{3,0,2,1:T(2,128)(2,1)S(1)}, bf16[1,1,32,2048]{3,0,2,1:T(2,128)(2,1)S(1)}, u32[]{:S(2)}, u32[]{:S(2)}) %collective-permute-start.7) | collective-permute-done | bytes 131104 | tf_op jit(solution)/shard_map/ppermute | solution.py:44
  174.1 1.7 collective-permute-done.6
  175.9 12.0 %collective-permute-done.5 = bf16[1,1,32,2048]{3,0,2,1:T(2,128)(2,1)S(1)} collective-permute-done((bf16[1,1,32,2048]{3,0,2,1:T(2,128)(2,1)S(1)}, bf16[1,1,32,2048]{3,0,2,1:T(2,128)(2,1)S(1)}, u32[]{:S(2)}, u32[]{:S(2)}) %collective-permute-start.5) | collective-permute-done | bytes 131104 | tf_op jit(solution)/shard_map/ppermute | solution.py:44
  187.9 3.0 collective-permute-done.4
  191.1 0.7 collective-permute-start.13
  191.8 7.3 %collective-permute-done = bf16[1,1,32,2048]{3,0,2,1:T(2,128)(2,1)S(1)} collective-permute-done((bf16[1,1,32,2048]{3,0,2,1:T(2,128)(2,1)S(1)}, bf16[1,1,32,2048]{3,0,2,1:T(2,128)(2,1)S(1)}, u32[]{:S(2)}, u32[]{:S(2)}) %collective-permute-start) | collective-permute-done | bytes 131104 | tf_op jit(solution)/shard_map/ppermute | solution.py:44
  199.2 0.6 copy-done.18
  200.3 4.3 dynamic_update_slice.45
  204.6 4.3 dynamic_update_slice.46
  208.9 4.3 dynamic_update_slice.47
  213.2 4.3 dynamic_update_slice.48
  217.5 4.3 dynamic_update_slice.49
  221.7 4.3 dynamic_update_slice.50
  226.0 4.3 dynamic_update_slice.51
  230.3 4.3 dynamic_update_slice.52
  234.6 4.3 dynamic_update_slice.53
  238.9 4.3 dynamic_update_slice.54
  243.2 4.3 dynamic_update_slice.55
  247.5 4.3 dynamic_update_slice.56
  251.8 4.3 dynamic_update_slice.57
  256.1 4.3 dynamic_update_slice.58
  260.4 4.3 dynamic_update_slice.59
  264.7 1.2 copy.35
  266.3 0.6 copy-done.8
  266.9 2.8 fusion.1
  269.7 5.2 %copy.54 = bf16[1,512,2048]{2,0,1:T(2,128)(2,1)} copy(bf16[1,512,2048]{2,1,0:T(8,128)(2,1)S(1)} %get-tuple-element.17) | data formatting | bytes 4194304 | tf_op jit(solution)/shard_map/broadcast_in_dim | solution.py:33
  274.9 13.2 %reduce.1 = bf16[512,2048]{1,0:T(8,128)(2,1)S(1)} reduce(bf16[512,1,2048]{2,1,0:T(2,128)(2,1)} %bitcast.63, bf16[]{:T(256)} %broadcast.39), dimensions={1}, to_apply=%bitcast.59.reduce_sub_computation | reduce | bytes 4194306
  288.0 2.8 reshape.97
  290.8 51.2 %all_to_all.33 = bf16[16,2,32768]{2,1,0:T(2,128)(2,1)S(1)} all-to-all(bf16[16,2,32768]{2,1,0:T(2,128)(2,1)} %reshape.97), channel_id=1, replica_groups=mesh['groups'=2,'seq'=16] {'seq'}, dimensions={0} | all-to-all | bytes 4194304 | tf_op jit(solution)/shard_map/all_to_all | solution.py:33
  342.0 6.8 %reshape.98 = bf16[512,1,2048]{2,1,0:T(2,128)(2,1)} reshape(bf16[16,2,32768]{2,1,0:T(2,128)(2,1)S(1)} %all_to_all.33) | data formatting | bytes 4194304
  348.7 3.5 copy.39
  352.2 2.4 fusion.4
  354.6 1.2 copy.30
  355.8 52.2 %all_to_all.34 = bf16[16,32,2048]{2,1,0:T(8,128)(2,1)S(1)} all-to-all(bf16[16,32,2048]{2,1,0:T(8,128)(2,1)S(1)} %copy.30), channel_id=1, replica_groups=mesh['groups'=2,'seq'=16] {'seq'}, dimensions={0} | all-to-all | bytes 4194304 | tf_op jit(solution)/shard_map/all_to_all | solution.py:55
  408.0 1.4 copy-done.6
  409.3 2.3 fusion.18
  411.7 4.0 fusion.11
  415.7 0.8 copy.38
  416.5 4.3 fusion.2
  420.8 4.1 copy.31
  424.9 6.1 %scatter_custom_fusion = bf16[512,2048]{1,0:T(8,128)(2,1)} fusion(s32[512]{0:T(512)S(1)} %compare_select_fusion, bf16[512,2048]{1,0:T(8,128)(2,1)} %copy.31, bf16[]{:T(256)} %constant.211.clone.1), kind=kCustom, calls=%fused_computation.21 | custom fusion | bytes 2097664 | tf_op jit(solution)/shard_map/scatter | solution.py:65
  431.1 74.5 %all-reduce.2.cloned.1.call-done = f32[512,512]{1,0:T(8,128)} async-done(((f32[512,512]{1,0:T(8,128)}), f32[512,512]{1,0:T(8,128)}) %all-reduce.2.cloned.1.call-update) | async-done | bytes 1048592 | tf_op jit(solution)/shard_map/psum | solution.py:61
  505.5 2.3 broadcast_multiply_fusion
  (62 shorter events, 2.1 us)
Async XLA Ops:
  7.2 1.6 copy-start
  8.8 3.3 copy-start.20
  39.3 8.2 %copy-start.19 = (bf16[32,16,16]{0,2,1:T(8,128)(2,1)S(1)}, bf16[32,16,16]{0,2,1:T(8,128)(2,1)}, u32[]{:S(2)}) copy-start(bf16[32,16,16]{0,2,1:T(8,128)(2,1)} %param.10) | copy-start | bytes 49156
  39.3 48.6 %all-to-all-start.2 = ((bf16[16,2,32768]{2,1,0:T(2,128)(2,1)}), bf16[16,2,32768]{2,1,0:T(2,128)(2,1)S(1)}, u32[]{:S(2)}, u32[]{:S(2)}) async-start(bf16[16,2,32768]{2,1,0:T(2,128)(2,1)} %reshape.95), calls=%async_computation.2 | async-start | bytes 4194304 | tf_op jit(solution)/shard_map/all_to_all | solution.py:32
  46.8 458.7 %all-reduce.2.cloned.1.call-start = ((), (), s32[]{:S(2)}) async-start(), calls=%async_computation.3 | async-start | bytes 2097152 | tf_op jit(solution)/shard_map/psum | solution.py:61
  98.2 1.4 copy-start.2
  107.0 16.1 %collective-permute-start.9 = (bf16[1,1,32,2048]{3,0,2,1:T(2,128)(2,1)S(1)}, bf16[1,1,32,2048]{3,0,2,1:T(2,128)(2,1)S(1)}, u32[]{:S(2)}, u32[]{:S(2)}) collective-permute-start(bf16[1,1,32,2048]{3,0,2,1:T(2,128)(2,1)S(1)} %get-tuple-element.23), channel_id=1, source_target_pairs={{0,10},{1,11},{2,12},{3,13},{4,14},{5,15},{6,0},{7,1},{8,2},{9,3},... | collective-permute-start | bytes 393224 | tf_op jit(solution)/shard_map/ppermute | solution.py:44
  115.6 26.2 %collective-permute-start.8 = (bf16[1,1,32,2048]{3,0,2,1:T(2,128)(2,1)S(1)}, bf16[1,1,32,2048]{3,0,2,1:T(2,128)(2,1)S(1)}, u32[]{:S(2)}, u32[]{:S(2)}) collective-permute-start(bf16[1,1,32,2048]{3,0,2,1:T(2,128)(2,1)S(1)} %get-tuple-element.24), channel_id=1, source_target_pairs={{0,9},{1,10},{2,11},{3,12},{4,13},{5,14},{6,15},{7,0},{8,1},{9,2},... | collective-permute-start | bytes 393224 | tf_op jit(solution)/shard_map/ppermute | solution.py:44
  115.7 58.4 %collective-permute-start.7 = (bf16[1,1,32,2048]{3,0,2,1:T(2,128)(2,1)S(1)}, bf16[1,1,32,2048]{3,0,2,1:T(2,128)(2,1)S(1)}, u32[]{:S(2)}, u32[]{:S(2)}) collective-permute-start(bf16[1,1,32,2048]{3,0,2,1:T(2,128)(2,1)S(1)} %get-tuple-element.25), channel_id=1, source_target_pairs={{0,8},{1,9},{2,10},{3,11},{4,12},{5,13},{6,14},{7,15},{8,0},{9,1},... | collective-permute-start | bytes 393224 | tf_op jit(solution)/shard_map/ppermute | solution.py:44
  117.5 58.4 %collective-permute-start.6 = (bf16[1,1,32,2048]{3,0,2,1:T(2,128)(2,1)S(1)}, bf16[1,1,32,2048]{3,0,2,1:T(2,128)(2,1)S(1)}, u32[]{:S(2)}, u32[]{:S(2)}) collective-permute-start(bf16[1,1,32,2048]{3,0,2,1:T(2,128)(2,1)S(1)} %get-tuple-element.26), channel_id=1, source_target_pairs={{0,7},{1,8},{2,9},{3,10},{4,11},{5,12},{6,13},{7,14},{8,15},{9,0},... | collective-permute-start | bytes 393224 | tf_op jit(solution)/shard_map/ppermute | solution.py:44
  118.8 69.1 %collective-permute-start.5 = (bf16[1,1,32,2048]{3,0,2,1:T(2,128)(2,1)S(1)}, bf16[1,1,32,2048]{3,0,2,1:T(2,128)(2,1)S(1)}, u32[]{:S(2)}, u32[]{:S(2)}) collective-permute-start(bf16[1,1,32,2048]{3,0,2,1:T(2,128)(2,1)S(1)} %get-tuple-element.27), channel_id=1, source_target_pairs={{0,6},{1,7},{2,8},{3,9},{4,10},{5,11},{6,12},{7,13},{8,14},{9,15},... | collective-permute-start | bytes 393224 | tf_op jit(solution)/shard_map/ppermute | solution.py:44
  123.1 76.0 %copy-start.9 = (bf16[1,1,32,2048]{3,0,2,1:T(2,128)(2,1)}, bf16[1,1,32,2048]{3,0,2,1:T(2,128)(2,1)S(1)}, u32[]{:S(2)}) copy-start(bf16[1,1,32,2048]{3,0,2,1:T(2,128)(2,1)S(1)} %collective-permute-done.9) | copy-start | bytes 393220
  123.1 67.8 %collective-permute-start.4 = (bf16[1,1,32,2048]{3,0,2,1:T(2,128)(2,1)S(1)}, bf16[1,1,32,2048]{3,0,2,1:T(2,128)(2,1)S(1)}, u32[]{:S(2)}, u32[]{:S(2)}) collective-permute-start(bf16[1,1,32,2048]{3,0,2,1:T(2,128)(2,1)S(1)} %get-tuple-element.28), channel_id=1, source_target_pairs={{0,5},{1,6},{2,7},{3,8},{4,9},{5,10},{6,11},{7,12},{8,13},{9,14},{... | collective-permute-start | bytes 393224 | tf_op jit(solution)/shard_map/ppermute | solution.py:44
  141.7 57.4 %copy-start.10 = (bf16[1,1,32,2048]{3,0,2,1:T(2,128)(2,1)}, bf16[1,1,32,2048]{3,0,2,1:T(2,128)(2,1)S(1)}, u32[]{:S(2)}) copy-start(bf16[1,1,32,2048]{3,0,2,1:T(2,128)(2,1)S(1)} %collective-permute-done.8) | copy-start | bytes 393220
  141.7 49.2 %collective-permute-start.3 = (bf16[1,1,32,2048]{3,0,2,1:T(2,128)(2,1)S(1)}, bf16[1,1,32,2048]{3,0,2,1:T(2,128)(2,1)S(1)}, u32[]{:S(2)}, u32[]{:S(2)}) collective-permute-start(bf16[1,1,32,2048]{3,0,2,1:T(2,128)(2,1)S(1)} %get-tuple-element.29), channel_id=1, source_target_pairs={{0,4},{1,5},{2,6},{3,7},{4,8},{5,9},{6,10},{7,11},{8,12},{9,13},{1... | collective-permute-start | bytes 393224 | tf_op jit(solution)/shard_map/ppermute | solution.py:44
  174.1 25.0 %copy-start.11 = (bf16[1,1,32,2048]{3,0,2,1:T(2,128)(2,1)}, bf16[1,1,32,2048]{3,0,2,1:T(2,128)(2,1)S(1)}, u32[]{:S(2)}) copy-start(bf16[1,1,32,2048]{3,0,2,1:T(2,128)(2,1)S(1)} %collective-permute-done.7) | copy-start | bytes 393220
  174.1 16.9 %collective-permute-start.2 = (bf16[1,1,32,2048]{3,0,2,1:T(2,128)(2,1)S(1)}, bf16[1,1,32,2048]{3,0,2,1:T(2,128)(2,1)S(1)}, u32[]{:S(2)}, u32[]{:S(2)}) collective-permute-start(bf16[1,1,32,2048]{3,0,2,1:T(2,128)(2,1)S(1)} %get-tuple-element.30), channel_id=1, source_target_pairs={{0,3},{1,4},{2,5},{3,6},{4,7},{5,8},{6,9},{7,10},{8,11},{9,12},{10... | collective-permute-start | bytes 393224 | tf_op jit(solution)/shard_map/ppermute | solution.py:44
  175.9 23.3 %copy-start.12 = (bf16[1,1,32,2048]{3,0,2,1:T(2,128)(2,1)}, bf16[1,1,32,2048]{3,0,2,1:T(2,128)(2,1)S(1)}, u32[]{:S(2)}) copy-start(bf16[1,1,32,2048]{3,0,2,1:T(2,128)(2,1)S(1)} %collective-permute-done.6) | copy-start | bytes 393220
  175.9 15.2 %collective-permute-start.1 = (bf16[1,1,32,2048]{3,0,2,1:T(2,128)(2,1)S(1)}, bf16[1,1,32,2048]{3,0,2,1:T(2,128)(2,1)S(1)}, u32[]{:S(2)}, u32[]{:S(2)}) collective-permute-start(bf16[1,1,32,2048]{3,0,2,1:T(2,128)(2,1)S(1)} %get-tuple-element.31), channel_id=1, source_target_pairs={{0,2},{1,3},{2,4},{3,5},{4,6},{5,7},{6,8},{7,9},{8,10},{9,11},{10,... | collective-permute-start | bytes 393224 | tf_op jit(solution)/shard_map/ppermute | solution.py:44
  187.9 11.2 %copy-start.13 = (bf16[1,1,32,2048]{3,0,2,1:T(2,128)(2,1)}, bf16[1,1,32,2048]{3,0,2,1:T(2,128)(2,1)S(1)}, u32[]{:S(2)}) copy-start(bf16[1,1,32,2048]{3,0,2,1:T(2,128)(2,1)S(1)} %collective-permute-done.5) | copy-start | bytes 393220
  187.9 11.2 %collective-permute-start = (bf16[1,1,32,2048]{3,0,2,1:T(2,128)(2,1)S(1)}, bf16[1,1,32,2048]{3,0,2,1:T(2,128)(2,1)S(1)}, u32[]{:S(2)}, u32[]{:S(2)}) collective-permute-start(bf16[1,1,32,2048]{3,0,2,1:T(2,128)(2,1)S(1)} %get-tuple-element.32), channel_id=1, source_target_pairs={{0,1},{1,2},{2,3},{3,4},{4,5},{5,6},{6,7},{7,8},{8,9},{9,10},{10,1... | collective-permute-start | bytes 393224 | tf_op jit(solution)/shard_map/ppermute | solution.py:44
  190.9 8.3 %copy-start.14 = (bf16[1,1,32,2048]{3,0,2,1:T(2,128)(2,1)}, bf16[1,1,32,2048]{3,0,2,1:T(2,128)(2,1)S(1)}, u32[]{:S(2)}) copy-start(bf16[1,1,32,2048]{3,0,2,1:T(2,128)(2,1)S(1)} %collective-permute-done.4) | copy-start | bytes 393220
  190.9 60.9 %collective-permute-start.12 = (bf16[1,1,32,2048]{3,0,2,1:T(2,128)(2,1)S(1)}, bf16[1,1,32,2048]{3,0,2,1:T(2,128)(2,1)}, u32[]{:S(2)}, u32[]{:S(2)}) collective-permute-start(bf16[1,1,32,2048]{3,0,2,1:T(2,128)(2,1)S(1)} %get-tuple-element.20), channel_id=1, source_target_pairs={{0,13},{1,14},{2,15},{3,0},{4,1},{5,2},{6,3},{7,4},{8,5},{9,6},{10... | collective-permute-start | bytes 393224 | tf_op jit(solution)/shard_map/ppermute | solution.py:44
  190.9 8.3 %copy-start.15 = (bf16[1,1,32,2048]{3,0,2,1:T(2,128)(2,1)}, bf16[1,1,32,2048]{3,0,2,1:T(2,128)(2,1)S(1)}, u32[]{:S(2)}) copy-start(bf16[1,1,32,2048]{3,0,2,1:T(2,128)(2,1)S(1)} %collective-permute-done.3) | copy-start | bytes 393220
  190.9 52.3 %collective-permute-start.10 = (bf16[1,1,32,2048]{3,0,2,1:T(2,128)(2,1)S(1)}, bf16[1,1,32,2048]{3,0,2,1:T(2,128)(2,1)}, u32[]{:S(2)}, u32[]{:S(2)}) collective-permute-start(bf16[1,1,32,2048]{3,0,2,1:T(2,128)(2,1)S(1)} %get-tuple-element.22), channel_id=1, source_target_pairs={{0,11},{1,12},{2,13},{3,14},{4,15},{5,0},{6,1},{7,2},{8,3},{9,4},{... | collective-permute-start | bytes 393224 | tf_op jit(solution)/shard_map/ppermute | solution.py:44
  191.0 8.2 %copy-start.16 = (bf16[1,1,32,2048]{3,0,2,1:T(2,128)(2,1)}, bf16[1,1,32,2048]{3,0,2,1:T(2,128)(2,1)S(1)}, u32[]{:S(2)}) copy-start(bf16[1,1,32,2048]{3,0,2,1:T(2,128)(2,1)S(1)} %collective-permute-done.2) | copy-start | bytes 393220
  191.0 56.5 %collective-permute-start.11 = (bf16[1,1,32,2048]{3,0,2,1:T(2,128)(2,1)S(1)}, bf16[1,1,32,2048]{3,0,2,1:T(2,128)(2,1)}, u32[]{:S(2)}, u32[]{:S(2)}) collective-permute-start(bf16[1,1,32,2048]{3,0,2,1:T(2,128)(2,1)S(1)} %get-tuple-element.21), channel_id=1, source_target_pairs={{0,12},{1,13},{2,14},{3,15},{4,0},{5,1},{6,2},{7,3},{8,4},{9,5},{1... | collective-permute-start | bytes 393224 | tf_op jit(solution)/shard_map/ppermute | solution.py:44
  191.1 8.1 %copy-start.17 = (bf16[1,1,32,2048]{3,0,2,1:T(2,128)(2,1)}, bf16[1,1,32,2048]{3,0,2,1:T(2,128)(2,1)S(1)}, u32[]{:S(2)}) copy-start(bf16[1,1,32,2048]{3,0,2,1:T(2,128)(2,1)S(1)} %collective-permute-done.1) | copy-start | bytes 393220
  191.1 65.0 %collective-permute-start.13 = (bf16[1,1,32,2048]{3,0,2,1:T(2,128)(2,1)S(1)}, bf16[1,1,32,2048]{3,0,2,1:T(2,128)(2,1)}, u32[]{:S(2)}, u32[]{:S(2)}) collective-permute-start(bf16[1,1,32,2048]{3,0,2,1:T(2,128)(2,1)S(1)} %get-tuple-element.19), channel_id=1, source_target_pairs={{0,14},{1,15},{2,0},{3,1},{4,2},{5,3},{6,4},{7,5},{8,6},{9,7},{10,... | collective-permute-start | bytes 393224 | tf_op jit(solution)/shard_map/ppermute | solution.py:44
  199.1 0.7 copy-start.18
  199.8 60.6 %collective-permute-start.14 = (bf16[1,1,32,2048]{3,0,2,1:T(2,128)(2,1)S(1)}, bf16[1,1,32,2048]{3,0,2,1:T(2,128)(2,1)}, u32[]{:S(2)}, u32[]{:S(2)}) collective-permute-start(bf16[1,1,32,2048]{3,0,2,1:T(2,128)(2,1)S(1)} %get-tuple-element.18), channel_id=1, source_target_pairs={{0,15},{1,0},{2,1},{3,2},{4,3},{5,4},{6,5},{7,6},{8,7},{9,8},{10,9... | collective-permute-start | bytes 393224 | tf_op jit(solution)/shard_map/ppermute | solution.py:44
  264.7 1.6 copy-start.7
  264.7 2.2 copy-start.8
  352.2 2.4 copy-start.4
  355.8 53.5 %copy-start.5 = (bf16[512,2048]{1,0:T(8,128)(2,1)S(1)}, bf16[512,2048]{1,0:T(8,128)(2,1)}, u32[]{:S(2)}) copy-start(bf16[512,2048]{1,0:T(8,128)(2,1)} %gather_fusion) | copy-start | bytes 6291460
  408.0 1.4 copy-start.6
  409.3 2.4 copy-start.3
  411.7 4.8 copy-start.21
  420.8 87.1 %copy-start.1 = (bf16[512,2048]{1,0:T(8,128)(2,1)S(1)}, bf16[512,2048]{1,0:T(8,128)(2,1)}, u32[]{:S(2)}) copy-start(bf16[512,2048]{1,0:T(8,128)(2,1)} %param.6) | copy-start | bytes 6291460
Sparse Core Ops, SparseCore 0:
  411.8 93.6 all-reduce.1
